TPU v7x, 256 devices: a whole 4x4x8 slice. The times are simulated.
256 devices in a mesh: gz: 64 (over x, z, core), gy: 4 (over y).
Axes of the slice: x: 4, y: 4, z: 8, core: 2. Of those that a mesh axis runs over, the one named last changes fastest.
Arguments:
- populations: float32 [19, 64, 128, 256], P(None, 'gz', 'gy'), may hold values from 0 to 0.5, as said below
- solid_fraction: float32 [64, 128, 256], P('gz', 'gy'), may hold values from 0 to 1
- labels: int32 [64, 128, 256], P('gz', 'gy'), may hold values from 0 to 4, as said below
Outputs:
- sensitivity: float32 [64, 128, 256], P('gz', 'gy')
- adjoint_populations: float32 [19, 64, 128, 256], P(None, 'gz', 'gy')
Inputs may be any that keep to these rules, and one draw needn't show every extreme that they name: `populations`: each population is w_q times a factor between 0.7 and 1.3. labels 3 appear only in the first plane along the feeding direction and 4 only in the last, in voxels that are not solid.
All inputs are finite; a program needn't handle non-finite values.
Results may differ from a plain program's by a relative error of at most 0.00028.
Values sent between devices are 32-bit elements; how exact they have to be, the bound alone decides.
A program may use at most 64 MiB of HBM per device.

v0:
```python
import jax
import jax.numpy as jnp
from jax import lax
from jax.sharding import PartitionSpec as P

STEPS = 2
OMEGA = 0.9
INLET_SPEED = 0.05


def padded_2(cells, sides, width):
    for axis, dim in sides:
        count = lax.axis_size(axis)
        head = lax.slice_in_dim(cells, 0, width, axis=dim)
        tail = lax.slice_in_dim(cells, cells.shape[dim] - width, cells.shape[dim], axis=dim)
        cells = jnp.concatenate(
            [
                lax.ppermute(tail, axis, [(i, (i + 1) % count) for i in range(count)]),
                cells,
                lax.ppermute(head, axis, [((i + 1) % count, i) for i in range(count)]),
            ],
            axis=dim,
        )
    return cells


def velocity_table():
    velocities = [(0, 0, 0)]
    for axis in range(3):
        for sign in (1, -1):
            vector = [0, 0, 0]
            vector[axis] = sign
            velocities.append(tuple(vector))
    for first in range(3):
        for second in range(first + 1, 3):
            for sign_a in (1, -1):
                for sign_b in (1, -1):
                    vector = [0, 0, 0]
                    vector[first] = sign_a
                    vector[second] = sign_b
                    velocities.append(tuple(vector))
    weights = [1.0 / 3.0] + [1.0 / 18.0] * 6 + [1.0 / 36.0] * 12
    opposite = [velocities.index(tuple((-e for e in vector))) for vector in velocities]
    return (velocities, weights, opposite)


def equilibrium(density, vel_x, vel_y, vel_z):
    velocities, weights, opposite = velocity_table()
    rows = []
    speed = vel_x * vel_x + vel_y * vel_y + vel_z * vel_z
    for index in range(19):
        cx, cy, cz = velocities[index]
        along = cx * vel_x + cy * vel_y + cz * vel_z
        rows.append(
            weights[index] * density * (1.0 + 3.0 * along + 4.5 * along * along - 1.5 * speed)
        )
    return jnp.stack(rows)


def moments(field):
    velocities, weights, opposite = velocity_table()
    density = jnp.sum(field, axis=0)
    mom_x = sum((velocities[q][0] * field[q] for q in range(19) if velocities[q][0] != 0))
    mom_y = sum((velocities[q][1] * field[q] for q in range(19) if velocities[q][1] != 0))
    mom_z = sum((velocities[q][2] * field[q] for q in range(19) if velocities[q][2] != 0))
    return (density, mom_x, mom_y, mom_z)


def collide(field, s_eff, labels):
    velocities, weights, opposite = velocity_table()
    density, mom_x, mom_y, mom_z = moments(field)
    feq = equilibrium(density, mom_x / density, mom_y / density, mom_z / density)
    rate = jnp.where(labels == 4, jnp.float32(1.0), jnp.float32(OMEGA))
    relaxed = field - rate * (field - feq)
    flipped = jnp.stack([field[opposite[q]] for q in range(19)])
    mixed = (1.0 - s_eff) * relaxed + s_eff * flipped
    ones = jnp.ones_like(density)
    inlet = equilibrium(ones, 0.0 * ones, 0.0 * ones, INLET_SPEED * ones)
    return jnp.where(labels == 3, inlet, mixed)


def energy(field, s_eff):
    density, mom_x, mom_y, mom_z = moments(field)
    return jnp.sum((1.0 - s_eff) * (mom_x * mom_x + mom_y * mom_y + mom_z * mom_z) / density)


def stream(field, sense):
    velocities, weights, opposite = velocity_table()
    depth = field.shape[1]
    height = field.shape[2]
    offsets = [(sense * v[0], sense * v[1], sense * v[2]) for v in velocities]
    padded = padded_2(field, (("gz", 1), ("gy", 2)), 1)
    moved = [
        padded[
            q,
            1 - offsets[q][2] : 1 - offsets[q][2] + depth,
            1 - offsets[q][1] : 1 - offsets[q][1] + height,
            :,
        ]
        for q in range(19)
    ]
    return jnp.stack([jnp.roll(moved[q], offsets[q][0], axis=2) for q in range(19)])


def global_energy(value):
    return lax.psum(value, ("gz", "gy"))


def on_device(populations, solid_fraction, labels):
    s_eff = jnp.where(
        labels == 1, solid_fraction, jnp.where(labels == 2, jnp.float32(1.0), jnp.float32(0.0))
    )
    states = [populations]
    total = jnp.float32(0.0)
    for step in range(STEPS):
        nxt = stream(collide(states[-1], s_eff, labels), 1)
        states.append(nxt)
        total = total + global_energy(energy(nxt, s_eff))
    energy_grad = jax.grad(energy, argnums=(0, 1))
    adjoint = jnp.zeros_like(populations)
    fraction_grad = jnp.zeros_like(solid_fraction)
    for step in reversed(range(STEPS)):
        grad_field, grad_frac = energy_grad(states[step + 1], s_eff)
        adjoint = adjoint + grad_field
        fraction_grad = fraction_grad + grad_frac
        pulled = stream(adjoint, -1)
        unused, pullback = jax.vjp(
            lambda field, frac: collide(field, frac, labels), states[step], s_eff
        )
        adjoint, grad_frac = pullback(pulled)
        fraction_grad = fraction_grad + grad_frac
    cells = (
        populations.shape[1]
        * populations.shape[2]
        * populations.shape[3]
        * lax.axis_size("gz")
        * lax.axis_size("gy")
    )
    mean_energy = total / (STEPS * cells)
    sensitivity = jnp.where(labels == 1, fraction_grad, jnp.float32(0.0)) / mean_energy
    return (sensitivity, adjoint / mean_energy)


def solution(mesh):
    in_specs = (P(None, "gz", "gy", None), P("gz", "gy", None), P("gz", "gy", None))
    out_specs = (P("gz", "gy", None), P(None, "gz", "gy", None))
    return jax.shard_map(
        on_device, mesh=mesh, in_specs=in_specs, out_specs=out_specs, check_vma=False
    )
```

profile of v0, /device:TPU:34, one launch (start us, length us, event | category | flops | bytes accessed | tf_op | source)
XLA Modules:
  0.0 174.0 jit_solution(15628574961668883643)
XLA Ops:
  1.5 1.1 reduce_sum.1999
  6.1 1.7 %collective-permute-start.1 = (f32[19,1,32,256]{3,2,1,0:T(8,128)S(1)}, f32[19,1,32,256]{3,2,1,0:T(8,128)S(1)}, u32[]{:S(2)}, u32[]{:S(2)}) collective-permute-start(f32[19,1,32,256]{3,2,1,0:T(8,128)S(1)} %add_select_fusion.1), channel_id=1, source_target_pairs={{4,0},{8,4},{12,8},{16,12},{20,16},{24,20},{28,24},{32,28},{36,32}... | collective-permute-start | bytes 1867784 | tf_op jit(solution)/shard_map/ppermute | solution.py:20
  8.1 7.6 %collective-permute-done.1 = f32[19,1,32,256]{3,2,1,0:T(8,128)S(1)} collective-permute-done((f32[19,1,32,256]{3,2,1,0:T(8,128)S(1)}, f32[19,1,32,256]{3,2,1,0:T(8,128)S(1)}, u32[]{:S(2)}, u32[]{:S(2)}) %collective-permute-start.1) | collective-permute-done | bytes 622624 | tf_op jit(solution)/shard_map/ppermute | solution.py:20
  15.9 1.7 collective-permute-start.2
  17.5 1.7 collective-permute-start.3
  19.3 2.1 %collective-permute-done.2 = f32[19,3,1,256]{3,2,1,0:T(1,128)S(1)} collective-permute-done((f32[19,3,1,256]{3,2,1,0:T(1,128)S(1)}, f32[19,3,1,256]{3,2,1,0:T(1,128)S(1)}, u32[]{:S(2)}, u32[]{:S(2)}) %collective-permute-start.2) | collective-permute-done | bytes 58400 | tf_op jit(solution)/shard_map/ppermute | solution.py:18
  26.1 1.0 collective-permute-start.5
  27.1 7.9 %collective-permute-done.4 = f32[19,1,32,256]{3,2,1,0:T(8,128)S(1)} collective-permute-done((f32[19,1,32,256]{3,2,1,0:T(8,128)S(1)}, f32[19,1,32,256]{3,2,1,0:T(8,128)S(1)}, u32[]{:S(2)}, u32[]{:S(2)}) %collective-permute-start.4) | collective-permute-done | bytes 622624 | tf_op jit(solution)/shard_map/ppermute | solution.py:18
  35.1 1.7 collective-permute-start.6
  36.7 1.7 collective-permute-start.7
  38.4 2.2 %collective-permute-done.6 = f32[19,3,1,256]{3,2,1,0:T(1,128)S(1)} collective-permute-done((f32[19,3,1,256]{3,2,1,0:T(1,128)S(1)}, f32[19,3,1,256]{3,2,1,0:T(1,128)S(1)}, u32[]{:S(2)}, u32[]{:S(2)}) %collective-permute-start.6) | collective-permute-done | bytes 58400 | tf_op jit(solution)/shard_map/ppermute | solution.py:18
  41.5 1.0 divide_reduce_fusion
  43.5 1.0 collective-permute-start.9
  44.7 7.7 %collective-permute-done.8 = f32[19,1,32,256]{3,2,1,0:T(8,128)S(1)} collective-permute-done((f32[19,1,32,256]{3,2,1,0:T(8,128)S(1)}, f32[19,1,32,256]{3,2,1,0:T(8,128)S(1)}, u32[]{:S(2)}, u32[]{:S(2)}) %collective-permute-start.8) | collective-permute-done | bytes 622624 | tf_op jit(solution)/shard_map/ppermute | solution.py:18
  52.5 3.1 %collective-permute-start.10 = (f32[19,3,1,256]{3,2,1,0:T(1,128)S(1)}, f32[19,3,1,256]{3,2,1,0:T(1,128)S(1)}, u32[]{:S(2)}, u32[]{:S(2)}) collective-permute-start(f32[19,3,1,256]{3,2,1,0:T(1,128)S(1)} %get-tuple-element.104), channel_id=1, source_target_pairs={{1,0},{2,1},{3,2},{0,3},{5,4},{6,5},{7,6},{4,7},{9,8},{10,9},{11,1... | collective-permute-start | bytes 175112 | tf_op jit(solution)/shard_map/ppermute | solution.py:20
  55.7 1.7 collective-permute-done.10
  57.5 3.6 %collective-permute-done.11 = f32[19,3,1,256]{3,2,1,0:T(1,128)S(1)} collective-permute-done((f32[19,3,1,256]{3,2,1,0:T(1,128)S(1)}, f32[19,3,1,256]{3,2,1,0:T(1,128)S(1)}, u32[]{:S(2)}, u32[]{:S(2)}) %collective-permute-start.11) | collective-permute-done | bytes 58400 | tf_op jit(solution)/shard_map/ppermute | solution.py:18
  65.1 1.4 collective-permute-start.12
  68.2 88.7 %psum.16 = f32[]{:T(128)} all-reduce(f32[]{:T(128)S(6)} %add.7467), channel_id=1, replica_groups=mesh['gz'=64,'gy'=4] {'gz','gy'}, use_global_device_ids=true, to_apply=%region_6.7 | all-reduce | flops 1 | bytes 8 | tf_op jit(solution)/shard_map/psum | solution.py:106
  157.9 3.0 %collective-permute-start.14 = (f32[19,3,1,256]{3,2,1,0:T(1,128)S(1)}, f32[19,3,1,256]{3,2,1,0:T(1,128)S(1)}, u32[]{:S(2)}, u32[]{:S(2)}) collective-permute-start(f32[19,3,1,256]{3,2,1,0:T(1,128)S(1)} %get-tuple-element.102), channel_id=1, source_target_pairs={{1,0},{2,1},{3,2},{0,3},{5,4},{6,5},{7,6},{4,7},{9,8},{10,9},{11,1... | collective-permute-start | bytes 175112 | tf_op jit(solution)/shard_map/ppermute | solution.py:20
  161.0 1.7 collective-permute-done.14
  162.8 3.6 %collective-permute-done.15 = f32[19,3,1,256]{3,2,1,0:T(1,128)S(1)} collective-permute-done((f32[19,3,1,256]{3,2,1,0:T(1,128)S(1)}, f32[19,3,1,256]{3,2,1,0:T(1,128)S(1)}, u32[]{:S(2)}, u32[]{:S(2)}) %collective-permute-start.15) | collective-permute-done | bytes 58400 | tf_op jit(solution)/shard_map/ppermute | solution.py:18
  167.7 1.0 copy-done.8
  172.9 1.1 add_divide_fusion
  (277 shorter events, 21.6 us)
Async XLA Ops:
  0.6 2.0 %copy-start = (f32[19,1,32,256]{3,2,1,0:T(8,128)S(1)}, f32[19,1,32,256]{3,2,1,0:T(8,128)}, u32[]{:S(2)}) copy-start(f32[19,1,32,256]{3,2,1,0:T(8,128)} %param.3) | copy-start | bytes 1867780
  6.1 9.7 %collective-permute-start = (f32[19,1,32,256]{3,2,1,0:T(8,128)S(1)}, f32[19,1,32,256]{3,2,1,0:T(8,128)S(1)}, u32[]{:S(2)}, u32[]{:S(2)}) collective-permute-start(f32[19,1,32,256]{3,2,1,0:T(8,128)S(1)} %add_select_fusion.1), channel_id=1, source_target_pairs={{0,4},{4,8},{8,12},{12,16},{16,20},{20,24},{24,28},{28,32},{32,36}... | collective-permute-start | bytes 1867784 | tf_op jit(solution)/shard_map/ppermute | solution.py:18
  6.1 9.5 %collective-permute-start.1 = (f32[19,1,32,256]{3,2,1,0:T(8,128)S(1)}, f32[19,1,32,256]{3,2,1,0:T(8,128)S(1)}, u32[]{:S(2)}, u32[]{:S(2)}) collective-permute-start(f32[19,1,32,256]{3,2,1,0:T(8,128)S(1)} %add_select_fusion.1), channel_id=1, source_target_pairs={{4,0},{8,4},{12,8},{16,12},{20,16},{24,20},{28,24},{32,28},{36,32}... | collective-permute-start | bytes 1867784 | tf_op jit(solution)/shard_map/ppermute | solution.py:20
  15.9 5.5 %collective-permute-start.2 = (f32[19,3,1,256]{3,2,1,0:T(1,128)S(1)}, f32[19,3,1,256]{3,2,1,0:T(1,128)S(1)}, u32[]{:S(2)}, u32[]{:S(2)}) collective-permute-start(f32[19,3,1,256]{3,2,1,0:T(1,128)S(1)} %get-tuple-element.111), channel_id=1, source_target_pairs={{0,1},{1,2},{2,3},{3,0},{4,5},{5,6},{6,7},{7,4},{8,9},{9,10},{10,1... | collective-permute-start | bytes 175112 | tf_op jit(solution)/shard_map/ppermute | solution.py:18
  17.5 4.2 %collective-permute-start.3 = (f32[19,3,1,256]{3,2,1,0:T(1,128)S(1)}, f32[19,3,1,256]{3,2,1,0:T(1,128)S(1)}, u32[]{:S(2)}, u32[]{:S(2)}) collective-permute-start(f32[19,3,1,256]{3,2,1,0:T(1,128)S(1)} %get-tuple-element.112), channel_id=1, source_target_pairs={{1,0},{2,1},{3,2},{0,3},{5,4},{6,5},{7,6},{4,7},{9,8},{10,9},{11,1... | collective-permute-start | bytes 175112 | tf_op jit(solution)/shard_map/ppermute | solution.py:20
  23.0 1.5 copy-start.5
  25.3 9.7 %collective-permute-start.4 = (f32[19,1,32,256]{3,2,1,0:T(8,128)S(1)}, f32[19,1,32,256]{3,2,1,0:T(8,128)S(1)}, u32[]{:S(2)}, u32[]{:S(2)}) collective-permute-start(f32[19,1,32,256]{3,2,1,0:T(8,128)S(1)} %add_select_fusion), channel_id=1, source_target_pairs={{0,4},{4,8},{8,12},{12,16},{16,20},{20,24},{24,28},{28,32},{32,36}... | collective-permute-start | bytes 1867784 | tf_op jit(solution)/shard_map/ppermute | solution.py:18
  26.1 8.9 %collective-permute-start.5 = (f32[19,1,32,256]{3,2,1,0:T(8,128)S(1)}, f32[19,1,32,256]{3,2,1,0:T(8,128)S(1)}, u32[]{:S(2)}, u32[]{:S(2)}) collective-permute-start(f32[19,1,32,256]{3,2,1,0:T(8,128)S(1)} %add_select_fusion), channel_id=1, source_target_pairs={{4,0},{8,4},{12,8},{16,12},{20,16},{24,20},{28,24},{32,28},{36,32}... | collective-permute-start | bytes 1867784 | tf_op jit(solution)/shard_map/ppermute | solution.py:20
  35.1 5.5 %collective-permute-start.6 = (f32[19,3,1,256]{3,2,1,0:T(1,128)S(1)}, f32[19,3,1,256]{3,2,1,0:T(1,128)S(1)}, u32[]{:S(2)}, u32[]{:S(2)}) collective-permute-start(f32[19,3,1,256]{3,2,1,0:T(1,128)S(1)} %get-tuple-element.107), channel_id=1, source_target_pairs={{0,1},{1,2},{2,3},{3,0},{4,5},{5,6},{6,7},{7,4},{8,9},{9,10},{10,1... | collective-permute-start | bytes 175112 | tf_op jit(solution)/shard_map/ppermute | solution.py:18
  36.7 4.2 %collective-permute-start.7 = (f32[19,3,1,256]{3,2,1,0:T(1,128)S(1)}, f32[19,3,1,256]{3,2,1,0:T(1,128)S(1)}, u32[]{:S(2)}, u32[]{:S(2)}) collective-permute-start(f32[19,3,1,256]{3,2,1,0:T(1,128)S(1)} %get-tuple-element.108), channel_id=1, source_target_pairs={{1,0},{2,1},{3,2},{0,3},{5,4},{6,5},{7,6},{4,7},{9,8},{10,9},{11,1... | collective-permute-start | bytes 175112 | tf_op jit(solution)/shard_map/ppermute | solution.py:20
  42.6 9.7 %collective-permute-start.8 = (f32[19,1,32,256]{3,2,1,0:T(8,128)S(1)}, f32[19,1,32,256]{3,2,1,0:T(8,128)S(1)}, u32[]{:S(2)}, u32[]{:S(2)}) collective-permute-start(f32[19,1,32,256]{3,2,1,0:T(8,128)S(1)} %add_add_fusion.1), channel_id=1, source_target_pairs={{0,4},{4,8},{8,12},{12,16},{16,20},{20,24},{24,28},{28,32},{32,36}... | collective-permute-start | bytes 1867784 | tf_op jit(solution)/shard_map/ppermute | solution.py:18
  43.5 8.9 %collective-permute-start.9 = (f32[19,1,32,256]{3,2,1,0:T(8,128)S(1)}, f32[19,1,32,256]{3,2,1,0:T(8,128)S(1)}, u32[]{:S(2)}, u32[]{:S(2)}) collective-permute-start(f32[19,1,32,256]{3,2,1,0:T(8,128)S(1)} %add_add_fusion.1), channel_id=1, source_target_pairs={{4,0},{8,4},{12,8},{16,12},{20,16},{24,20},{28,24},{32,28},{36,32}... | collective-permute-start | bytes 1867784 | tf_op jit(solution)/shard_map/ppermute | solution.py:20
  52.5 5.0 %collective-permute-start.10 = (f32[19,3,1,256]{3,2,1,0:T(1,128)S(1)}, f32[19,3,1,256]{3,2,1,0:T(1,128)S(1)}, u32[]{:S(2)}, u32[]{:S(2)}) collective-permute-start(f32[19,3,1,256]{3,2,1,0:T(1,128)S(1)} %get-tuple-element.104), channel_id=1, source_target_pairs={{1,0},{2,1},{3,2},{0,3},{5,4},{6,5},{7,6},{4,7},{9,8},{10,9},{11,1... | collective-permute-start | bytes 175112 | tf_op jit(solution)/shard_map/ppermute | solution.py:20
  55.7 5.4 %collective-permute-start.11 = (f32[19,3,1,256]{3,2,1,0:T(1,128)S(1)}, f32[19,3,1,256]{3,2,1,0:T(1,128)S(1)}, u32[]{:S(2)}, u32[]{:S(2)}) collective-permute-start(f32[19,3,1,256]{3,2,1,0:T(1,128)S(1)} %get-tuple-element.103), channel_id=1, source_target_pairs={{0,1},{1,2},{2,3},{3,0},{4,5},{5,6},{6,7},{7,4},{8,9},{9,10},{10,1... | collective-permute-start | bytes 175112 | tf_op jit(solution)/shard_map/ppermute | solution.py:18
  62.3 1.8 %copy-start.1 = (f32[19,1,32,256]{3,2,1,0:T(8,128)}, f32[19,1,32,256]{3,2,1,0:T(8,128)S(1)}, u32[]{:S(2)}) copy-start(f32[19,1,32,256]{3,2,1,0:T(8,128)S(1)} %constant_dynamic-update-slice_fusion.108) | copy-start | bytes 1867780
  65.1 92.7 %collective-permute-start.12 = (f32[19,1,32,256]{3,2,1,0:T(8,128)S(1)}, f32[19,1,32,256]{3,2,1,0:T(8,128)S(1)}, u32[]{:S(2)}, u32[]{:S(2)}) collective-permute-start(f32[19,1,32,256]{3,2,1,0:T(8,128)S(1)} %add_add_fusion), channel_id=1, source_target_pairs={{0,4},{4,8},{8,12},{12,16},{16,20},{20,24},{24,28},{28,32},{32,36}... | collective-permute-start | bytes 1867784 | tf_op jit(solution)/shard_map/ppermute | solution.py:18
  66.5 91.3 %collective-permute-start.13 = (f32[19,1,32,256]{3,2,1,0:T(8,128)S(1)}, f32[19,1,32,256]{3,2,1,0:T(8,128)S(1)}, u32[]{:S(2)}, u32[]{:S(2)}) collective-permute-start(f32[19,1,32,256]{3,2,1,0:T(8,128)S(1)} %add_add_fusion), channel_id=1, source_target_pairs={{4,0},{8,4},{12,8},{16,12},{20,16},{24,20},{28,24},{32,28},{36,32}... | collective-permute-start | bytes 1867784 | tf_op jit(solution)/shard_map/ppermute | solution.py:20
  157.9 4.9 %collective-permute-start.14 = (f32[19,3,1,256]{3,2,1,0:T(1,128)S(1)}, f32[19,3,1,256]{3,2,1,0:T(1,128)S(1)}, u32[]{:S(2)}, u32[]{:S(2)}) collective-permute-start(f32[19,3,1,256]{3,2,1,0:T(1,128)S(1)} %get-tuple-element.102), channel_id=1, source_target_pairs={{1,0},{2,1},{3,2},{0,3},{5,4},{6,5},{7,6},{4,7},{9,8},{10,9},{11,1... | collective-permute-start | bytes 175112 | tf_op jit(solution)/shard_map/ppermute | solution.py:20
  161.0 5.4 %collective-permute-start.15 = (f32[19,3,1,256]{3,2,1,0:T(1,128)S(1)}, f32[19,3,1,256]{3,2,1,0:T(1,128)S(1)}, u32[]{:S(2)}, u32[]{:S(2)}) collective-permute-start(f32[19,3,1,256]{3,2,1,0:T(1,128)S(1)} %get-tuple-element.101), channel_id=1, source_target_pairs={{0,1},{1,2},{2,3},{3,0},{4,5},{5,6},{6,7},{7,4},{8,9},{9,10},{10,1... | collective-permute-start | bytes 175112 | tf_op jit(solution)/shard_map/ppermute | solution.py:18
  167.6 1.1 copy-start.8
  167.6 1.3 copy-start.10
  167.7 1.4 copy-start.2
  167.7 1.6 copy-start.4
  167.7 1.8 %copy-start.6 = (f32[19,1,32,256]{3,2,1,0:T(8,128)S(1)}, f32[19,1,32,256]{3,2,1,0:T(8,128)}, u32[]{:S(2)}) copy-start(f32[19,1,32,256]{3,2,1,0:T(8,128)} %copy-done.5) | copy-start | bytes 1867780
  (7 other events, 5.6 us)
where the time goes:
time: 174 us
  blocking collectives  88.7 us (51%)
  waiting for transfers between devices  38.5 us (22%)
  starting transfers between devices  20 us (11%)
  other arithmetic  13.8 us (8%)
  local copies, waits for them, and re-layouts  9.47 us (5%)
  between operations  3.68 us (2%)
    psum x1, blocking collectives, global_energy(): return lax.psum(value, ('gz', 'gy'))  88.7 us
    ppermute x8, waiting for transfers between devices, padded_2(): lax.ppermute(tail, axis, [(i, (i + 1) % count) for i in range(count)])  27 us
    ppermute x8, starting transfers between devices, padded_2(): lax.ppermute(head, axis, [((i + 1) % count, i) for i in range(count)])  13.7 us
    ppermute x8, waiting for transfers between devices, padded_2(): lax.ppermute(head, axis, [((i + 1) % count, i) for i in range(count)])  11.5 us
    ppermute x8, starting transfers between devices, padded_2(): lax.ppermute(tail, axis, [(i, (i + 1) % count) for i in range(count)])  6.31 us
    unnamed x76, local copies, waits for them, and re-layouts  6.28 us
    unnamed x79, other arithmetic  4.62 us
  transfers between devices with their start and end apart: 16, of which 12 were waited for; matrix products, arithmetic and copies ran while one was open for 1% of the time, Pallas kernels for 0%

commit v1 on v0

--- a/solution.py
+++ b/solution.py
@@ -103,7 +103,7 @@
 
 
 def global_energy(value):
-    return lax.psum(value, ("gz", "gy"))
+    return lax.psum(lax.psum(value, "gy"), "gz")
 
 
 def on_device(populations, solid_fraction, labels):

time: 174 us -> 233 us (1.34)
  the two profiles are of different devices: /device:TPU:34 before, /device:TPU:1 now
where the time goes in v1:
time: 233 us; the launch traced here: 232 us
  blocking collectives  137 us (59%)
  starting transfers between devices  39.7 us (17%)
  waiting for transfers between devices  28.6 us (12%)
  other arithmetic  13.8 us (6%)
  local copies, waits for them, and re-layouts  9.46 us (4%)
  between operations  3.66 us (2%)
    psum x2, blocking collectives, global_energy(): return lax.psum(lax.psum(value, 'gy'), 'gz')  137 us
    ppermute x8, starting transfers between devices, padded_2(): lax.ppermute(head, axis, [((i + 1) % count, i) for i in range(count)])  30.6 us
    ppermute x8, waiting for transfers between devices, padded_2(): lax.ppermute(head, axis, [((i + 1) % count, i) for i in range(count)])  15.3 us
    ppermute x8, waiting for transfers between devices, padded_2(): lax.ppermute(tail, axis, [(i, (i + 1) % count) for i in range(count)])  13.4 us
    ppermute x8, starting transfers between devices, padded_2(): lax.ppermute(tail, axis, [(i, (i + 1) % count) for i in range(count)])  9.08 us
    unnamed x76, local copies, waits for them, and re-layouts  6.27 us
  transfers between devices with their start and end apart: 16, of which 11 were waited for; matrix products, arithmetic and copies ran while one was open for 1% of the time, Pallas kernels for 0%

profile of v1, /device:TPU:1, one launch (start us, length us, event | category | flops | bytes accessed | tf_op | source)
XLA Modules:
  0.0 232.4 jit_solution(702206534442771621)
XLA Ops:
  6.1 3.0 %collective-permute-start = (f32[19,1,32,256]{3,2,1,0:T(8,128)S(1)}, f32[19,1,32,256]{3,2,1,0:T(8,128)S(1)}, u32[]{:S(2)}, u32[]{:S(2)}) collective-permute-start(f32[19,1,32,256]{3,2,1,0:T(8,128)S(1)} %add_select_fusion.1), channel_id=1, source_target_pairs={{0,4},{4,8},{8,12},{12,16},{16,20},{20,24},{24,28},{28,32},{32,36}... | collective-permute-start | bytes 1867784 | tf_op jit(solution)/shard_map/ppermute | solution.py:18
  9.5 9.6 %collective-permute-done.1 = f32[19,1,32,256]{3,2,1,0:T(8,128)S(1)} collective-permute-done((f32[19,1,32,256]{3,2,1,0:T(8,128)S(1)}, f32[19,1,32,256]{3,2,1,0:T(8,128)S(1)}, u32[]{:S(2)}, u32[]{:S(2)}) %collective-permute-start.1) | collective-permute-done | bytes 622624 | tf_op jit(solution)/shard_map/ppermute | solution.py:20
  19.3 1.4 collective-permute-start.2
  20.7 1.5 collective-permute-start.3
  22.3 1.4 collective-permute-done.2
  28.3 4.2 %collective-permute-start.5 = (f32[19,1,32,256]{3,2,1,0:T(8,128)S(1)}, f32[19,1,32,256]{3,2,1,0:T(8,128)S(1)}, u32[]{:S(2)}, u32[]{:S(2)}) collective-permute-start(f32[19,1,32,256]{3,2,1,0:T(8,128)S(1)} %add_select_fusion), channel_id=1, source_target_pairs={{4,0},{8,4},{12,8},{16,12},{20,16},{24,20},{28,24},{32,28},{36,32}... | collective-permute-start | bytes 1867784 | tf_op jit(solution)/shard_map/ppermute | solution.py:20
  32.6 3.0 %collective-permute-done.4 = f32[19,1,32,256]{3,2,1,0:T(8,128)S(1)} collective-permute-done((f32[19,1,32,256]{3,2,1,0:T(8,128)S(1)}, f32[19,1,32,256]{3,2,1,0:T(8,128)S(1)}, u32[]{:S(2)}, u32[]{:S(2)}) %collective-permute-start.4) | collective-permute-done | bytes 622624 | tf_op jit(solution)/shard_map/ppermute | solution.py:18
  35.5 2.5 %collective-permute-done.5 = f32[19,1,32,256]{3,2,1,0:T(8,128)S(1)} collective-permute-done((f32[19,1,32,256]{3,2,1,0:T(8,128)S(1)}, f32[19,1,32,256]{3,2,1,0:T(8,128)S(1)}, u32[]{:S(2)}, u32[]{:S(2)}) %collective-permute-start.5) | collective-permute-done | bytes 622624 | tf_op jit(solution)/shard_map/ppermute | solution.py:20
  38.1 1.4 collective-permute-start.6
  39.5 1.4 collective-permute-start.7
  40.9 1.9 collective-permute-done.6
  45.7 7.6 %collective-permute-start.9 = (f32[19,1,32,256]{3,2,1,0:T(8,128)S(1)}, f32[19,1,32,256]{3,2,1,0:T(8,128)S(1)}, u32[]{:S(2)}, u32[]{:S(2)}) collective-permute-start(f32[19,1,32,256]{3,2,1,0:T(8,128)S(1)} %add_add_fusion.1), channel_id=1, source_target_pairs={{4,0},{8,4},{12,8},{16,12},{20,16},{24,20},{28,24},{32,28},{36,32}... | collective-permute-start | bytes 1867784 | tf_op jit(solution)/shard_map/ppermute | solution.py:20
  53.6 1.2 collective-permute-done.8
  55.5 2.8 %collective-permute-start.10 = (f32[19,3,1,256]{3,2,1,0:T(1,128)S(1)}, f32[19,3,1,256]{3,2,1,0:T(1,128)S(1)}, u32[]{:S(2)}, u32[]{:S(2)}) collective-permute-start(f32[19,3,1,256]{3,2,1,0:T(1,128)S(1)} %get-tuple-element.104), channel_id=1, source_target_pairs={{1,0},{2,1},{3,2},{0,3},{5,4},{6,5},{7,6},{4,7},{9,8},{10,9},{11,1... | collective-permute-start | bytes 175112 | tf_op jit(solution)/shard_map/ppermute | solution.py:20
  58.4 1.2 collective-permute-done.10
  59.7 3.3 %collective-permute-done.11 = f32[19,3,1,256]{3,2,1,0:T(1,128)S(1)} collective-permute-done((f32[19,3,1,256]{3,2,1,0:T(1,128)S(1)}, f32[19,3,1,256]{3,2,1,0:T(1,128)S(1)}, u32[]{:S(2)}, u32[]{:S(2)}) %collective-permute-start.11) | collective-permute-done | bytes 58400 | tf_op jit(solution)/shard_map/ppermute | solution.py:18
  67.0 1.2 collective-permute-start.12
  68.2 11.0 %collective-permute-start.13 = (f32[19,1,32,256]{3,2,1,0:T(8,128)S(1)}, f32[19,1,32,256]{3,2,1,0:T(8,128)S(1)}, u32[]{:S(2)}, u32[]{:S(2)}) collective-permute-start(f32[19,1,32,256]{3,2,1,0:T(8,128)S(1)} %add_add_fusion), channel_id=1, source_target_pairs={{4,0},{8,4},{12,8},{16,12},{20,16},{24,20},{28,24},{32,28},{36,32}... | collective-permute-start | bytes 1867784 | tf_op jit(solution)/shard_map/ppermute | solution.py:20
  80.4 7.2 %psum.33 = f32[]{:T(128)} all-reduce(f32[]{:T(128)S(6)} %add.7471), channel_id=1, replica_groups=mesh['gz'=64,'gy'=4] {'gy'}, use_global_device_ids=true, to_apply=%region_6.7 | all-reduce | flops 1 | bytes 8 | tf_op jit(solution)/shard_map/psum | solution.py:106
  87.6 130.1 %psum.32 = f32[]{:T(128)} all-reduce(f32[]{:T(128)} %psum.33), channel_id=1, replica_groups=mesh['gz'=64,'gy'=4] {'gz'}, use_global_device_ids=true, to_apply=%region_7.8 | all-reduce | flops 1 | bytes 8 | tf_op jit(solution)/shard_map/psum | solution.py:106
  218.7 1.8 collective-permute-start.14
  220.6 1.5 collective-permute-done.14
  222.1 2.7 %collective-permute-done.15 = f32[19,3,1,256]{3,2,1,0:T(1,128)S(1)} collective-permute-done((f32[19,3,1,256]{3,2,1,0:T(1,128)S(1)}, f32[19,3,1,256]{3,2,1,0:T(1,128)S(1)}, u32[]{:S(2)}, u32[]{:S(2)}) %collective-permute-start.15) | collective-permute-done | bytes 58400 | tf_op jit(solution)/shard_map/ppermute | solution.py:18
  231.3 1.1 add_divide_fusion
  (278 shorter events, 25.0 us)
Async XLA Ops:
  0.6 2.0 copy-start
  6.1 13.1 %collective-permute-start = (f32[19,1,32,256]{3,2,1,0:T(8,128)S(1)}, f32[19,1,32,256]{3,2,1,0:T(8,128)S(1)}, u32[]{:S(2)}, u32[]{:S(2)}) collective-permute-start(f32[19,1,32,256]{3,2,1,0:T(8,128)S(1)} %add_select_fusion.1), channel_id=1, source_target_pairs={{0,4},{4,8},{8,12},{12,16},{16,20},{20,24},{24,28},{28,32},{32,36}... | collective-permute-start | bytes 1867784 | tf_op jit(solution)/shard_map/ppermute | solution.py:18
  9.1 10.0 %collective-permute-start.1 = (f32[19,1,32,256]{3,2,1,0:T(8,128)S(1)}, f32[19,1,32,256]{3,2,1,0:T(8,128)S(1)}, u32[]{:S(2)}, u32[]{:S(2)}) collective-permute-start(f32[19,1,32,256]{3,2,1,0:T(8,128)S(1)} %add_select_fusion.1), channel_id=1, source_target_pairs={{4,0},{8,4},{12,8},{16,12},{20,16},{24,20},{28,24},{32,28},{36,32}... | collective-permute-start | bytes 1867784 | tf_op jit(solution)/shard_map/ppermute | solution.py:20
  19.3 4.4 %collective-permute-start.2 = (f32[19,3,1,256]{3,2,1,0:T(1,128)S(1)}, f32[19,3,1,256]{3,2,1,0:T(1,128)S(1)}, u32[]{:S(2)}, u32[]{:S(2)}) collective-permute-start(f32[19,3,1,256]{3,2,1,0:T(1,128)S(1)} %get-tuple-element.111), channel_id=1, source_target_pairs={{0,1},{1,2},{2,3},{3,0},{4,5},{5,6},{6,7},{7,4},{8,9},{9,10},{10,1... | collective-permute-start | bytes 175112 | tf_op jit(solution)/shard_map/ppermute | solution.py:18
  20.7 3.0 %collective-permute-start.3 = (f32[19,3,1,256]{3,2,1,0:T(1,128)S(1)}, f32[19,3,1,256]{3,2,1,0:T(1,128)S(1)}, u32[]{:S(2)}, u32[]{:S(2)}) collective-permute-start(f32[19,3,1,256]{3,2,1,0:T(1,128)S(1)} %get-tuple-element.112), channel_id=1, source_target_pairs={{1,0},{2,1},{3,2},{0,3},{5,4},{6,5},{7,6},{4,7},{9,8},{10,9},{11,1... | collective-permute-start | bytes 175112 | tf_op jit(solution)/shard_map/ppermute | solution.py:20
  25.0 1.5 copy-start.5
  27.3 8.2 %collective-permute-start.4 = (f32[19,1,32,256]{3,2,1,0:T(8,128)S(1)}, f32[19,1,32,256]{3,2,1,0:T(8,128)S(1)}, u32[]{:S(2)}, u32[]{:S(2)}) collective-permute-start(f32[19,1,32,256]{3,2,1,0:T(8,128)S(1)} %add_select_fusion), channel_id=1, source_target_pairs={{0,4},{4,8},{8,12},{12,16},{16,20},{20,24},{24,28},{28,32},{32,36}... | collective-permute-start | bytes 1867784 | tf_op jit(solution)/shard_map/ppermute | solution.py:18
  28.3 9.7 %collective-permute-start.5 = (f32[19,1,32,256]{3,2,1,0:T(8,128)S(1)}, f32[19,1,32,256]{3,2,1,0:T(8,128)S(1)}, u32[]{:S(2)}, u32[]{:S(2)}) collective-permute-start(f32[19,1,32,256]{3,2,1,0:T(8,128)S(1)} %add_select_fusion), channel_id=1, source_target_pairs={{4,0},{8,4},{12,8},{16,12},{20,16},{24,20},{28,24},{32,28},{36,32}... | collective-permute-start | bytes 1867784 | tf_op jit(solution)/shard_map/ppermute | solution.py:20
  38.1 4.6 %collective-permute-start.6 = (f32[19,3,1,256]{3,2,1,0:T(1,128)S(1)}, f32[19,3,1,256]{3,2,1,0:T(1,128)S(1)}, u32[]{:S(2)}, u32[]{:S(2)}) collective-permute-start(f32[19,3,1,256]{3,2,1,0:T(1,128)S(1)} %get-tuple-element.107), channel_id=1, source_target_pairs={{0,1},{1,2},{2,3},{3,0},{4,5},{5,6},{6,7},{7,4},{8,9},{9,10},{10,1... | collective-permute-start | bytes 175112 | tf_op jit(solution)/shard_map/ppermute | solution.py:18
  39.5 3.5 %collective-permute-start.7 = (f32[19,3,1,256]{3,2,1,0:T(1,128)S(1)}, f32[19,3,1,256]{3,2,1,0:T(1,128)S(1)}, u32[]{:S(2)}, u32[]{:S(2)}) collective-permute-start(f32[19,3,1,256]{3,2,1,0:T(1,128)S(1)} %get-tuple-element.108), channel_id=1, source_target_pairs={{1,0},{2,1},{3,2},{0,3},{5,4},{6,5},{7,6},{4,7},{9,8},{10,9},{11,1... | collective-permute-start | bytes 175112 | tf_op jit(solution)/shard_map/ppermute | solution.py:20
  44.7 10.1 %collective-permute-start.8 = (f32[19,1,32,256]{3,2,1,0:T(8,128)S(1)}, f32[19,1,32,256]{3,2,1,0:T(8,128)S(1)}, u32[]{:S(2)}, u32[]{:S(2)}) collective-permute-start(f32[19,1,32,256]{3,2,1,0:T(8,128)S(1)} %add_add_fusion.1), channel_id=1, source_target_pairs={{0,4},{4,8},{8,12},{12,16},{16,20},{20,24},{24,28},{28,32},{32,36}... | collective-permute-start | bytes 1867784 | tf_op jit(solution)/shard_map/ppermute | solution.py:18
  45.7 9.7 %collective-permute-start.9 = (f32[19,1,32,256]{3,2,1,0:T(8,128)S(1)}, f32[19,1,32,256]{3,2,1,0:T(8,128)S(1)}, u32[]{:S(2)}, u32[]{:S(2)}) collective-permute-start(f32[19,1,32,256]{3,2,1,0:T(8,128)S(1)} %add_add_fusion.1), channel_id=1, source_target_pairs={{4,0},{8,4},{12,8},{16,12},{20,16},{24,20},{28,24},{32,28},{36,32}... | collective-permute-start | bytes 1867784 | tf_op jit(solution)/shard_map/ppermute | solution.py:20
  55.5 4.1 %collective-permute-start.10 = (f32[19,3,1,256]{3,2,1,0:T(1,128)S(1)}, f32[19,3,1,256]{3,2,1,0:T(1,128)S(1)}, u32[]{:S(2)}, u32[]{:S(2)}) collective-permute-start(f32[19,3,1,256]{3,2,1,0:T(1,128)S(1)} %get-tuple-element.104), channel_id=1, source_target_pairs={{1,0},{2,1},{3,2},{0,3},{5,4},{6,5},{7,6},{4,7},{9,8},{10,9},{11,1... | collective-permute-start | bytes 175112 | tf_op jit(solution)/shard_map/ppermute | solution.py:20
  58.4 4.6 %collective-permute-start.11 = (f32[19,3,1,256]{3,2,1,0:T(1,128)S(1)}, f32[19,3,1,256]{3,2,1,0:T(1,128)S(1)}, u32[]{:S(2)}, u32[]{:S(2)}) collective-permute-start(f32[19,3,1,256]{3,2,1,0:T(1,128)S(1)} %get-tuple-element.103), channel_id=1, source_target_pairs={{0,1},{1,2},{2,3},{3,0},{4,5},{5,6},{6,7},{7,4},{8,9},{9,10},{10,1... | collective-permute-start | bytes 175112 | tf_op jit(solution)/shard_map/ppermute | solution.py:18
  64.2 1.8 copy-start.1
  67.0 151.6 %collective-permute-start.12 = (f32[19,1,32,256]{3,2,1,0:T(8,128)S(1)}, f32[19,1,32,256]{3,2,1,0:T(8,128)S(1)}, u32[]{:S(2)}, u32[]{:S(2)}) collective-permute-start(f32[19,1,32,256]{3,2,1,0:T(8,128)S(1)} %add_add_fusion), channel_id=1, source_target_pairs={{0,4},{4,8},{8,12},{12,16},{16,20},{20,24},{24,28},{28,32},{32,36}... | collective-permute-start | bytes 1867784 | tf_op jit(solution)/shard_map/ppermute | solution.py:18
  68.2 150.4 %collective-permute-start.13 = (f32[19,1,32,256]{3,2,1,0:T(8,128)S(1)}, f32[19,1,32,256]{3,2,1,0:T(8,128)S(1)}, u32[]{:S(2)}, u32[]{:S(2)}) collective-permute-start(f32[19,1,32,256]{3,2,1,0:T(8,128)S(1)} %add_add_fusion), channel_id=1, source_target_pairs={{4,0},{8,4},{12,8},{16,12},{20,16},{24,20},{28,24},{32,28},{36,32}... | collective-permute-start | bytes 1867784 | tf_op jit(solution)/shard_map/ppermute | solution.py:20
  218.7 3.4 %collective-permute-start.14 = (f32[19,3,1,256]{3,2,1,0:T(1,128)S(1)}, f32[19,3,1,256]{3,2,1,0:T(1,128)S(1)}, u32[]{:S(2)}, u32[]{:S(2)}) collective-permute-start(f32[19,3,1,256]{3,2,1,0:T(1,128)S(1)} %get-tuple-element.102), channel_id=1, source_target_pairs={{1,0},{2,1},{3,2},{0,3},{5,4},{6,5},{7,6},{4,7},{9,8},{10,9},{11,1... | collective-permute-start | bytes 175112 | tf_op jit(solution)/shard_map/ppermute | solution.py:20
  220.5 4.3 %collective-permute-start.15 = (f32[19,3,1,256]{3,2,1,0:T(1,128)S(1)}, f32[19,3,1,256]{3,2,1,0:T(1,128)S(1)}, u32[]{:S(2)}, u32[]{:S(2)}) collective-permute-start(f32[19,3,1,256]{3,2,1,0:T(1,128)S(1)} %get-tuple-element.101), channel_id=1, source_target_pairs={{0,1},{1,2},{2,3},{3,0},{4,5},{5,6},{6,7},{7,4},{8,9},{9,10},{10,1... | collective-permute-start | bytes 175112 | tf_op jit(solution)/shard_map/ppermute | solution.py:18
  226.0 1.1 copy-start.8
  226.0 1.3 copy-start.10
  226.1 1.4 copy-start.2
  226.1 1.6 copy-start.4
  226.1 1.8 copy-start.6
  (7 other events, 5.6 us)
